TPU v7x, 32 devices: a whole 2x2x4 slice. The times are simulated.
32 devices in a mesh: dp: 2 (over x), expert: 16 (over z, y, core).
Axes of the slice: x: 2, y: 2, z: 4, core: 2. Of those that a mesh axis runs over, the one named last changes fastest.
Arguments:
- saved_inputs: bfloat16 [1024, 3584], P('expert'), may hold values from -6 to 6
- output_grad: bfloat16 [1024, 3584], P('expert'), may hold values from -6 to 6
- routes: int32 [1024, 8], P('expert'), may hold values from 0 to 15, all different within a row; in each aligned block of 64 rows (0 to 63, 64 to 127, ...) at most 36 rows name the same one
- route_gates: bfloat16 [1024, 8], P('expert'), may hold values from 0.099609375 to 1
- expert_gate: bfloat16 [16, 3584, 1024], P('expert', None, 'dp'), may hold values from -0.09375 to 0.09375
- expert_up: bfloat16 [16, 3584, 1024], P('expert', None, 'dp'), may hold values from -0.09375 to 0.09375
- expert_down: bfloat16 [16, 1024, 3584], P('expert', 'dp'), may hold values from -0.1875 to 0.1875
- proj_basis: bfloat16 [16, 1024, 128], P('expert', 'dp'), may hold values from -0.1875 to 0.1875
Outputs:
- input_grad: bfloat16 [1024, 3584], P('expert', 'dp')
- projected: float32 [16, 3584, 3, 128], P('expert', 'dp')
Inputs may be any that keep to these rules, and one draw needn't show every extreme that they name: Within each aligned block of 64 tokens no expert is named by more than 36 routes, and in every draw some expert is named by exactly 36.
All inputs are finite; a program needn't handle non-finite values.
Results may differ from a plain program's by a relative error of at most 0.009.
Values may be sent and summed in bfloat16 or wider, within the bound.
A program may use at most 128 MiB of HBM per device.

v0:
```python
import jax
import jax.numpy as jnp
from jax import lax
from jax.sharding import PartitionSpec as P


def on_device(
    saved_inputs, output_grad, routes, route_gates, expert_gate, expert_up, expert_down, proj_basis
):
    token_count, model_width = saved_inputs.shape
    top_count = routes.shape[1]
    expert_count = lax.axis_size("expert")
    group_count = lax.axis_size("dp")
    capacity = token_count * top_count * 9 // (8 * expert_count)
    slot_count = expert_count * capacity
    column_width = model_width // group_count
    route_count = token_count * top_count
    flat_routes = routes.reshape(-1)
    one_hot = (flat_routes[:, None] == jnp.arange(expert_count, dtype=jnp.int32)[None, :]).astype(
        jnp.int32
    )
    earlier = jnp.sum((jnp.cumsum(one_hot, axis=0) - one_hot) * one_hot, axis=1)
    target_slot = flat_routes * capacity + earlier
    slot_owner = (
        jnp.full((slot_count,), route_count, jnp.int32)
        .at[target_slot]
        .set(jnp.arange(route_count, dtype=jnp.int32))
    )
    filled = slot_owner < route_count
    safe_route = jnp.minimum(slot_owner, route_count - 1)
    source_token = safe_route // top_count
    zero_half = jnp.zeros((), jnp.bfloat16)
    gate_slots = jnp.where(filled, route_gates.reshape(-1)[safe_route], zero_half).reshape(
        expert_count, capacity
    )
    token_map = (
        (source_token[None, :] == jnp.arange(token_count, dtype=jnp.int32)[:, None])
        & filled[None, :]
    ).astype(jnp.bfloat16)
    contract_first = (((0,), (0,)), ((), ()))

    def to_slots(source_rows):
        picked = lax.dot_general(
            token_map, source_rows, contract_first, preferred_element_type=jnp.float32
        ).astype(jnp.bfloat16)
        return picked.reshape(expert_count, capacity * source_rows.shape[1])

    recv_inputs, recv_grads, recv_gates = (
        lax.all_to_all(to_slots(saved_inputs), "expert", split_axis=0, concat_axis=0, tiled=True),
        lax.all_to_all(to_slots(output_grad), "expert", split_axis=0, concat_axis=0, tiled=True),
        lax.all_to_all(gate_slots, "expert", split_axis=0, concat_axis=0, tiled=True),
    )
    input_rows = recv_inputs.reshape(slot_count, model_width)
    grad_rows = recv_grads.reshape(slot_count, model_width)
    gain = recv_gates.reshape(slot_count, 1).astype(jnp.float32)
    gate_w = expert_gate[0]
    up_w = expert_up[0]
    down_w = expert_down[0]
    basis = proj_basis[0]
    rank_width = basis.shape[1]
    contract_last = (((1,), (1,)), ((), ()))
    pre_gate = jnp.dot(input_rows, gate_w, preferred_element_type=jnp.float32)
    pre_up = jnp.dot(input_rows, up_w, preferred_element_type=jnp.float32)
    grad_hidden = lax.dot_general(
        grad_rows, down_w, contract_last, preferred_element_type=jnp.float32
    )
    sigma = jax.nn.sigmoid(pre_gate)
    silu_val = pre_gate * sigma
    scaled = gain * grad_hidden
    grad_up = (scaled * silu_val).astype(jnp.bfloat16)
    grad_gate = (scaled * pre_up * sigma * (1.0 + pre_gate * (1.0 - sigma))).astype(jnp.bfloat16)
    hidden = (silu_val * pre_up).astype(jnp.bfloat16)
    part_rows = (
        lax.dot_general(grad_gate, gate_w, contract_last, preferred_element_type=jnp.float32)
        + lax.dot_general(grad_up, up_w, contract_last, preferred_element_type=jnp.float32)
    ).astype(jnp.bfloat16)
    coef_gate = jnp.dot(grad_gate, basis, preferred_element_type=jnp.float32).astype(jnp.bfloat16)
    coef_up = jnp.dot(grad_up, basis, preferred_element_type=jnp.float32).astype(jnp.bfloat16)
    coef_down = (gain * jnp.dot(hidden, basis, preferred_element_type=jnp.float32)).astype(
        jnp.bfloat16
    )
    coef_pair = jnp.concatenate([coef_gate, coef_up], axis=1)
    front = lax.dot_general(
        input_rows, coef_pair, contract_first, preferred_element_type=jnp.float32
    )
    rear = lax.dot_general(grad_rows, coef_down, contract_first, preferred_element_type=jnp.float32)
    summed_terms = lax.psum_scatter(
        jnp.concatenate([front, rear], axis=1).astype(jnp.bfloat16),
        "dp",
        scatter_dimension=0,
        tiled=True,
    ).astype(jnp.float32)
    projected = summed_terms.reshape(1, column_width, 3, rank_width)
    returned = lax.all_to_all(
        part_rows.reshape(expert_count, capacity * model_width),
        "expert",
        split_axis=0,
        concat_axis=0,
        tiled=True,
    )
    spread = jnp.dot(
        token_map, returned.reshape(slot_count, model_width), preferred_element_type=jnp.float32
    )
    token_grad = lax.psum_scatter(
        spread.astype(jnp.bfloat16), "dp", scatter_dimension=1, tiled=True
    )
    return (token_grad, projected)


def solution(mesh):
    placed = (
        P("expert", None),
        P("expert", None),
        P("expert", None),
        P("expert", None),
        P("expert", None, "dp"),
        P("expert", None, "dp"),
        P("expert", "dp", None),
        P("expert", "dp", None),
    )
    return jax.shard_map(
        on_device,
        mesh=mesh,
        in_specs=placed,
        out_specs=(P("expert", "dp"), P("expert", "dp", None, None)),
        check_vma=False,
    )
```

profile of v0, /device:TPU:0, one launch (start us, length us, event | category | flops | bytes accessed | tf_op | source)
XLA Modules:
  0.0 535.4 jit_solution(17826223306023978186)
XLA Ops:
  14.0 3.9 gather_fusion
  18.6 7.4 %all-to-all-start = ((bf16[16,1,36]{2,1,0:T(2,128)(2,1)}), bf16[16,1,36]{2,1,0:T(2,128)(2,1)S(1)}, u32[]{:S(2)}, u32[]{:S(2)}) async-start(bf16[16,1,36]{2,1,0:T(2,128)(2,1)} %all_to_all.32), calls=%async_computation | async-start | bytes 16384 | tf_op jit(solution)/shard_map/all_to_all | solution.py:51
  29.3 7.9 %all_to_all.34 = bf16[16,1,129024]{2,1,0:T(2,128)(2,1)} reshape(bf16[576,3584]{1,0:T(8,128)(2,1)} %convolution_convert_fusion) | data formatting | bytes 8257536 | tf_op jit(solution)/shard_map/all_to_all | solution.py:49
  37.8 26.8 %reduce.9 = bf16[16,129024]{1,0:T(8,128)(2,1)} reduce(bf16[16,1,129024]{2,1,0:T(2,128)(2,1)} %all_to_all.34, bf16[]{:T(256)} %broadcast.86), dimensions={1}, to_apply=%all_to_all.34.reduce_sub_computation | reduce | bytes 8257538 | tf_op jit(solution)/shard_map/all_to_all | solution.py:49
  64.6 6.6 %reshape.140 = bf16[16,2,64512]{2,1,0:T(2,128)(2,1)} reshape(bf16[16,129024]{1,0:T(8,128)(2,1)} %reduce.9) | data formatting | bytes 8257536
  71.2 6.4 %all-to-all-start.2 = ((bf16[16,2,64512]{2,1,0:T(2,128)(2,1)}), bf16[16,2,64512]{2,1,0:T(2,128)(2,1)}, u32[]{:S(2)}, u32[]{:S(2)}) async-start(bf16[16,2,64512]{2,1,0:T(2,128)(2,1)} %reshape.140), calls=%async_computation.2 | async-start | bytes 8257536 | tf_op jit(solution)/shard_map/all_to_all | solution.py:49
  80.8 7.9 %all_to_all.33 = bf16[16,1,129024]{2,1,0:T(2,128)(2,1)} reshape(bf16[576,3584]{1,0:T(8,128)(2,1)} %convolution_convert_fusion.1) | data formatting | bytes 8257536 | tf_op jit(solution)/shard_map/all_to_all | solution.py:50
  88.7 26.7 %reduce.10 = bf16[16,129024]{1,0:T(8,128)(2,1)} reduce(bf16[16,1,129024]{2,1,0:T(2,128)(2,1)} %all_to_all.33, bf16[]{:T(256)} %broadcast.86), dimensions={1}, to_apply=%all_to_all.33.reduce_sub_computation | reduce | bytes 8257538 | tf_op jit(solution)/shard_map/all_to_all | solution.py:50
  115.5 6.6 %reshape.142 = bf16[16,2,64512]{2,1,0:T(2,128)(2,1)} reshape(bf16[16,129024]{1,0:T(8,128)(2,1)} %reduce.10) | data formatting | bytes 8257536
  122.0 31.9 %all-to-all-done.2 = bf16[16,2,64512]{2,1,0:T(2,128)(2,1)} async-done(((bf16[16,2,64512]{2,1,0:T(2,128)(2,1)}), bf16[16,2,64512]{2,1,0:T(2,128)(2,1)}, u32[]{:S(2)}, u32[]{:S(2)}) %all-to-all-start.2) | async-done | bytes 4128800 | tf_op jit(solution)/shard_map/all_to_all | solution.py:49
  154.0 19.7 %all-to-all-start.1 = ((bf16[16,2,64512]{2,1,0:T(2,128)(2,1)}), bf16[16,2,64512]{2,1,0:T(2,128)(2,1)}, u32[]{:S(2)}, u32[]{:S(2)}) async-start(bf16[16,2,64512]{2,1,0:T(2,128)(2,1)} %reshape.142), calls=%async_computation.1 | async-start | bytes 8257536 | tf_op jit(solution)/shard_map/all_to_all | solution.py:50
  173.8 12.2 %reshape.141 = bf16[16,1,129024]{2,1,0:T(2,128)(2,1)} reshape(bf16[16,2,64512]{2,1,0:T(2,128)(2,1)} %all-to-all-done.2) | data formatting | bytes 8257536
  186.0 26.1 %reduce.3 = bf16[16,129024]{1,0:T(8,128)(2,1)} reduce(bf16[16,1,129024]{2,1,0:T(2,128)(2,1)} %reshape.141, bf16[]{:T(256)} %constant.41), dimensions={1}, to_apply=%all_to_all.29.reduce_sub_computation | reduce | bytes 8257538 | tf_op jit(solution)/shard_map/all_to_all | solution.py:49
  212.0 9.0 %reshape.103 = bf16[576,3584]{1,0:T(8,128)(2,1)} reshape(bf16[16,129024]{1,0:T(8,128)(2,1)} %reduce.3) | data formatting | bytes 8257536 | tf_op jit(solution)/shard_map/reshape | solution.py:53
  221.1 5.7 %fusion.2 = f32[576,512]{1,0:T(8,128)S(1)} fusion(bf16[576,3584]{1,0:T(8,128)(2,1)} %reshape.103, bf16[1,3584,512]{2,1,0:T(8,128)(2,1)} %param.12), kind=kOutput, calls=%fused_computation.10 | convolution fusion | flops 2113929216 | bytes 8978432 | tf_op jit(solution)/shard_map/dot_general | solution.py:62
  230.1 19.9 %all-to-all-done.1 = bf16[16,2,64512]{2,1,0:T(2,128)(2,1)} async-done(((bf16[16,2,64512]{2,1,0:T(2,128)(2,1)}), bf16[16,2,64512]{2,1,0:T(2,128)(2,1)}, u32[]{:S(2)}, u32[]{:S(2)}) %all-to-all-start.1) | async-done | bytes 4128800 | tf_op jit(solution)/shard_map/all_to_all | solution.py:50
  250.1 12.2 %reshape.143 = bf16[16,1,129024]{2,1,0:T(2,128)(2,1)} reshape(bf16[16,2,64512]{2,1,0:T(2,128)(2,1)} %all-to-all-done.1) | data formatting | bytes 8257536
  262.2 26.1 %reduce.2 = bf16[16,129024]{1,0:T(8,128)(2,1)} reduce(bf16[16,1,129024]{2,1,0:T(2,128)(2,1)} %reshape.143, bf16[]{:T(256)} %constant.41), dimensions={1}, to_apply=%all_to_all.27.reduce_sub_computation | reduce | bytes 8257538 | tf_op jit(solution)/shard_map/all_to_all | solution.py:50
  288.3 9.5 %reshape.102 = bf16[576,3584]{1,0:T(8,128)(2,1)} reshape(bf16[16,129024]{1,0:T(8,128)(2,1)} %reduce.2) | data formatting | bytes 8257536 | tf_op jit(solution)/shard_map/reshape | solution.py:54
  297.8 6.4 %multiply_convert_fusion.1 = (bf16[576,512]{1,0:T(8,128)(2,1)S(1)}, bf16[576,512]{1,0:T(8,128)(2,1)S(1)}) fusion(f32[576,512]{1,0:T(8,128)S(1)} %fusion.2, f32[576,512]{1,0:T(8,128)} %fusion.5, bf16[576,3584]{1,0:T(8,128)(2,1)} %reshape.102, bf16[1,512,3584]{2,1,0:T(8,128)(2,1)} %param.14, f32[576]{0:T(1024)S(1)} %reshape.107), kind=kOutput, calls=%fused_computation.20 | convolution fusion | flops 2118057984 | bytes 11340032 | tf_op jit(solution)/shard_map/dot_general | solution.py:64
  306.6 4.4 add_convert_fusion
  311.0 7.9 %all_to_all.35 = bf16[16,1,129024]{2,1,0:T(2,128)(2,1)} reshape(bf16[576,3584]{1,0:T(8,128)(2,1)} %add_convert_fusion) | data formatting | bytes 8257536 | tf_op jit(solution)/shard_map/all_to_all | solution.py:94
  318.9 26.8 %reduce.11 = bf16[16,129024]{1,0:T(8,128)(2,1)} reduce(bf16[16,1,129024]{2,1,0:T(2,128)(2,1)} %all_to_all.35, bf16[]{:T(256)} %broadcast.86), dimensions={1}, to_apply=%all_to_all.35.reduce_sub_computation | reduce | bytes 8257538 | tf_op jit(solution)/shard_map/all_to_all | solution.py:94
  345.7 6.7 %reshape.144 = bf16[16,2,64512]{2,1,0:T(2,128)(2,1)} reshape(bf16[16,129024]{1,0:T(8,128)(2,1)} %reduce.11) | data formatting | bytes 8257536
  352.4 19.5 %all-to-all-start.3 = ((bf16[16,2,64512]{2,1,0:T(2,128)(2,1)}), bf16[16,2,64512]{2,1,0:T(2,128)(2,1)}, u32[]{:S(2)}, u32[]{:S(2)}) async-start(bf16[16,2,64512]{2,1,0:T(2,128)(2,1)} %reshape.144), calls=%async_computation.3 | async-start | bytes 8257536 | tf_op jit(solution)/shard_map/all_to_all | solution.py:94
  376.4 4.3 convolution_convert_fusion.3
  382.5 65.8 %all-to-all-done.3 = bf16[16,2,64512]{2,1,0:T(2,128)(2,1)} async-done(((bf16[16,2,64512]{2,1,0:T(2,128)(2,1)}), bf16[16,2,64512]{2,1,0:T(2,128)(2,1)}, u32[]{:S(2)}, u32[]{:S(2)}) %all-to-all-start.3) | async-done | bytes 4128800 | tf_op jit(solution)/shard_map/all_to_all | solution.py:94
  448.3 12.2 %reshape.145 = bf16[16,1,129024]{2,1,0:T(2,128)(2,1)} reshape(bf16[16,2,64512]{2,1,0:T(2,128)(2,1)} %all-to-all-done.3) | data formatting | bytes 8257536
  460.5 26.1 %reduce.4 = bf16[16,129024]{1,0:T(8,128)(2,1)} reduce(bf16[16,1,129024]{2,1,0:T(2,128)(2,1)} %reshape.145, bf16[]{:T(256)} %constant.41), dimensions={1}, to_apply=%all_to_all.31.reduce_sub_computation | reduce | bytes 8257538 | tf_op jit(solution)/shard_map/all_to_all | solution.py:94
  486.6 9.1 %reshape.104 = bf16[576,3584]{1,0:T(8,128)(2,1)} reshape(bf16[16,129024]{1,0:T(8,128)(2,1)} %reduce.4) | data formatting | bytes 8257536 | tf_op jit(solution)/shard_map/reshape | solution.py:102
  495.7 3.8 convolution_convert_fusion.4
  502.5 25.9 %reduce-scatter.3.cloned.1.call-done = bf16[64,1792]{1,0:T(8,128)(2,1)} async-done(((bf16[64,3584]{1,0:T(8,128)(2,1)}), bf16[64,1792]{1,0:T(8,128)(2,1)}) %reduce-scatter.3.cloned.1.call-update) | async-done | bytes 229392 | tf_op jit(solution)/shard_map/reduce_scatter | solution.py:104
  (57 shorter events, 29.5 us)
Async XLA Ops:
  7.2 18.9 %copy-start = (bf16[64,3584]{1,0:T(8,128)(2,1)S(1)}, bf16[64,3584]{1,0:T(8,128)(2,1)}, u32[]{:S(2)}) copy-start(bf16[64,3584]{1,0:T(8,128)(2,1)} %param.8) | copy-start | bytes 1376260
  18.6 52.6 %all-to-all-start = ((bf16[16,1,36]{2,1,0:T(2,128)(2,1)}), bf16[16,1,36]{2,1,0:T(2,128)(2,1)S(1)}, u32[]{:S(2)}, u32[]{:S(2)}) async-start(bf16[16,1,36]{2,1,0:T(2,128)(2,1)} %all_to_all.32), calls=%async_computation | async-start | bytes 16384 | tf_op jit(solution)/shard_map/all_to_all | solution.py:51
  71.2 6.4 %copy-start.4 = (bf16[64,3584]{1,0:T(8,128)(2,1)S(1)}, bf16[64,3584]{1,0:T(8,128)(2,1)}, u32[]{:S(2)}) copy-start(bf16[64,3584]{1,0:T(8,128)(2,1)} %param.9) | copy-start | bytes 1376260
  71.2 82.8 %all-to-all-start.2 = ((bf16[16,2,64512]{2,1,0:T(2,128)(2,1)}), bf16[16,2,64512]{2,1,0:T(2,128)(2,1)}, u32[]{:S(2)}, u32[]{:S(2)}) async-start(bf16[16,2,64512]{2,1,0:T(2,128)(2,1)} %reshape.140), calls=%async_computation.2 | async-start | bytes 8257536 | tf_op jit(solution)/shard_map/all_to_all | solution.py:49
  154.0 96.1 %all-to-all-start.1 = ((bf16[16,2,64512]{2,1,0:T(2,128)(2,1)}), bf16[16,2,64512]{2,1,0:T(2,128)(2,1)}, u32[]{:S(2)}, u32[]{:S(2)}) async-start(bf16[16,2,64512]{2,1,0:T(2,128)(2,1)} %reshape.142), calls=%async_computation.1 | async-start | bytes 8257536 | tf_op jit(solution)/shard_map/all_to_all | solution.py:50
  221.1 5.7 %copy-start.2 = (bf16[576,3584]{1,0:T(8,128)(2,1)S(1)}, bf16[576,3584]{1,0:T(8,128)(2,1)}, u32[]{:S(2)}) copy-start(bf16[576,3584]{1,0:T(8,128)(2,1)} %reshape.103) | copy-start | bytes 12386308
  221.1 5.7 %copy-start.6 = (bf16[1,3584,512]{2,1,0:T(8,128)(2,1)S(1)}, bf16[1,3584,512]{2,1,0:T(8,128)(2,1)}, u32[]{:S(2)}) copy-start(bf16[1,3584,512]{2,1,0:T(8,128)(2,1)} %param.13) | copy-start | bytes 11010052
  226.8 71.0 %copy-start.8 = (f32[576,512]{1,0:T(8,128)}, f32[576,512]{1,0:T(8,128)S(1)}, u32[]{:S(2)}) copy-start(f32[576,512]{1,0:T(8,128)S(1)} %fusion.2) | copy-start | bytes 3538948
  297.8 6.4 %copy-start.5 = (bf16[1,3584,512]{2,1,0:T(8,128)(2,1)S(1)}, bf16[1,3584,512]{2,1,0:T(8,128)(2,1)}, u32[]{:S(2)}) copy-start(bf16[1,3584,512]{2,1,0:T(8,128)(2,1)} %param.12) | copy-start | bytes 11010052
  304.2 2.4 copy-start.7
  352.4 19.6 %copy-start.3 = (bf16[1,512,128]{2,1,0:T(8,128)(2,1)S(1)}, bf16[1,512,128]{2,1,0:T(8,128)(2,1)}, u32[]{:S(2)}) copy-start(bf16[1,512,128]{2,1,0:T(8,128)(2,1)} %param.15) | copy-start | bytes 393220
  352.4 96.0 %all-to-all-start.3 = ((bf16[16,2,64512]{2,1,0:T(2,128)(2,1)}), bf16[16,2,64512]{2,1,0:T(2,128)(2,1)}, u32[]{:S(2)}, u32[]{:S(2)}) async-start(bf16[16,2,64512]{2,1,0:T(2,128)(2,1)} %reshape.144), calls=%async_computation.3 | async-start | bytes 8257536 | tf_op jit(solution)/shard_map/all_to_all | solution.py:94
  371.9 127.6 %reduce-scatter.5.cloned.1.call-start = ((), (), s32[]{:S(2)}) async-start(), calls=%async_computation.7 | async-start | bytes 4128768 | tf_op jit(solution)/shard_map/reduce_scatter | solution.py:87
  382.4 145.9 %reduce-scatter.3.cloned.1.call-start = ((), (), s32[]{:S(2)}) async-start(), calls=%async_computation.6 | async-start | bytes 688128 | tf_op jit(solution)/shard_map/reduce_scatter | solution.py:104
  486.6 41.7 %copy-start.1 = (bf16[64,3584]{1,0:T(8,128)(2,1)S(1)}, bf16[64,3584]{1,0:T(8,128)(2,1)}, u32[]{:S(2)}) copy-start(bf16[64,3584]{1,0:T(8,128)(2,1)} %param.8) | copy-start | bytes 1376260
Sparse Core Ops, SparseCore 0:
  382.6 40.3 reduce-scatter.4
  499.7 28.6 reduce-scatter.2
where the time goes:
time: 543 us; the launch traced here: 535 us
  other arithmetic  162 us (30%)
  waiting for transfers between devices  144 us (27%)
  local copies, waits for them, and re-layouts  121 us (22%)
  starting transfers between devices  53.1 us (10%)
  matrix products  41.1 us (8%)
  between operations  14.5 us (3%)
    all_to_all x1, waiting for transfers between devices, on_device(): lax.all_to_all(part_rows.reshape(expert_count, capacity * model_width), '...  65.8 us
    unnamed x27, local copies, waits for them, and re-layouts  60.9 us
    all_to_all x2, other arithmetic, on_device(): lax.all_to_all(part_rows.reshape(expert_count, capacity * model_width), '...  52.9 us
    all_to_all x2, other arithmetic, on_device(): lax.all_to_all(to_slots(saved_inputs), 'expert', split_axis=0, concat_axi...  52.8 us
    all_to_all x2, other arithmetic, on_device(): lax.all_to_all(to_slots(output_grad), 'expert', split_axis=0, concat_axis...  52.8 us
    all_to_all x1, waiting for transfers between devices, on_device(): lax.all_to_all(to_slots(saved_inputs), 'expert', split_axis=0, concat_axi...  31.9 us
    reduce_scatter x1, waiting for transfers between devices, on_device(): lax.psum_scatter(spread.astype(jnp.bfloat16), 'dp', scatter_dimension=1,...  25.9 us
    all_to_all x1, waiting for transfers between devices, on_device(): lax.all_to_all(to_slots(output_grad), 'expert', split_axis=0, concat_axis...  19.9 us
  transfers between devices with their start and end apart: 6, of which 4 were waited for; matrix products, arithmetic and copies ran while one was open for 36% of the time, Pallas kernels for 0%

commit v1 on v0

--- a/solution.py
+++ b/solution.py
@@ -4,7 +4,7 @@
 from jax.sharding import PartitionSpec as P
 
 
-def on_device(
+def slot_form(
     saved_inputs, output_grad, routes, route_gates, expert_gate, expert_up, expert_down, proj_basis
 ):
     token_count, model_width = saved_inputs.shape
@@ -107,6 +107,75 @@
     return (token_grad, projected)
 
 
+def dense_form(
+    saved_inputs, output_grad, routes, route_gates, expert_gate, expert_up, expert_down, proj_basis
+):
+    model_width = saved_inputs.shape[1]
+    expert_count = lax.axis_size("expert")
+    group_count = lax.axis_size("dp")
+    column_width = model_width // group_count
+    experts = jnp.arange(expert_count, dtype=jnp.int32)
+    chosen = routes[:, :, None] == experts[None, None, :]
+    gate_table = jnp.sum(
+        jnp.where(chosen, route_gates.astype(jnp.float32)[:, :, None], 0.0), axis=1
+    ).astype(jnp.bfloat16)
+    all_gates = lax.all_gather(gate_table, "expert", axis=0, tiled=True)
+    input_rows = lax.all_gather(saved_inputs, "expert", axis=0, tiled=True)
+    grad_rows = lax.all_gather(output_grad, "expert", axis=0, tiled=True)
+    own = experts == lax.axis_index("expert")
+    gain = jnp.sum(
+        jnp.where(own[None, :], all_gates.astype(jnp.float32), 0.0), axis=1, keepdims=True
+    )
+    gate_w = expert_gate[0]
+    up_w = expert_up[0]
+    down_w = expert_down[0]
+    basis = proj_basis[0]
+    rank_width = basis.shape[1]
+    contract_first = (((0,), (0,)), ((), ()))
+    contract_last = (((1,), (1,)), ((), ()))
+    pre_gate = jnp.dot(input_rows, gate_w, preferred_element_type=jnp.float32)
+    pre_up = jnp.dot(input_rows, up_w, preferred_element_type=jnp.float32)
+    grad_hidden = lax.dot_general(
+        grad_rows, down_w, contract_last, preferred_element_type=jnp.float32
+    )
+    sigma = jax.nn.sigmoid(pre_gate)
+    silu_val = pre_gate * sigma
+    scaled = gain * grad_hidden
+    grad_up = (scaled * silu_val).astype(jnp.bfloat16)
+    grad_gate = (scaled * pre_up * sigma * (1.0 + pre_gate * (1.0 - sigma))).astype(jnp.bfloat16)
+    hidden = (silu_val * pre_up).astype(jnp.bfloat16)
+    part_rows = (
+        lax.dot_general(grad_gate, gate_w, contract_last, preferred_element_type=jnp.float32)
+        + lax.dot_general(grad_up, up_w, contract_last, preferred_element_type=jnp.float32)
+    ).astype(jnp.bfloat16)
+    own_rows = lax.psum_scatter(part_rows, "expert", scatter_dimension=0, tiled=True)
+    token_grad = lax.psum_scatter(own_rows, "dp", scatter_dimension=1, tiled=True)
+    coef_gate = jnp.dot(grad_gate, basis, preferred_element_type=jnp.float32).astype(jnp.bfloat16)
+    coef_up = jnp.dot(grad_up, basis, preferred_element_type=jnp.float32).astype(jnp.bfloat16)
+    coef_down = (gain * jnp.dot(hidden, basis, preferred_element_type=jnp.float32)).astype(
+        jnp.bfloat16
+    )
+    coef_pair = jnp.concatenate([coef_gate, coef_up], axis=1)
+    front = lax.dot_general(
+        input_rows, coef_pair, contract_first, preferred_element_type=jnp.float32
+    )
+    rear = lax.dot_general(grad_rows, coef_down, contract_first, preferred_element_type=jnp.float32)
+    summed_terms = lax.psum_scatter(
+        jnp.concatenate([front, rear], axis=1).astype(jnp.bfloat16),
+        "dp",
+        scatter_dimension=0,
+        tiled=True,
+    ).astype(jnp.float32)
+    projected = summed_terms.reshape(1, column_width, 3, rank_width)
+    return (token_grad, projected)
+
+
+def on_device(*arrays):
+    if lax.axis_size("expert") <= 2 * arrays[2].shape[1]:
+        return dense_form(*arrays)
+    return slot_form(*arrays)
+
+
 def solution(mesh):
     placed = (
         P("expert", None),

time: 543 us -> 332 us (0.61); the launches traced: 535 us -> 332 us
  other arithmetic: 162 us -> 3.19 us
  local copies, waits for them, and re-layouts: 121 us -> 3.04 us
  waiting for transfers between devices: 144 us -> 232 us
  starting transfers between devices: 53.1 us -> 0.38 us
  blocking collectives: 0 us -> 23.8 us
  matrix products: 41.1 us -> 55.2 us
    all_to_all x6 -> x0, other arithmetic: 159 us -> none  [the longest x2 52.9 us: on_device(): lax.all_to_all(part_rows.reshape(expert_count, capacity * model_width), '...]
    all_to_all x4 -> x0, waiting for transfers between devices: 118 us -> none  [the longest x1 65.8 us: on_device(): lax.all_to_all(part_rows.reshape(expert_count, capacity * model_width), '...]
    reduce_scatter x2 -> x3, waiting for transfers between devices: 25.9 us -> 130 us  [the longest x1 75 us: dense_form(): lax.psum_scatter(part_rows, 'expert', scatter_dimension=0, tiled=True)]
    all_gather x0 -> x2, waiting for transfers between devices: none -> 101 us  [the longest x1 53.9 us: dense_form(): grad_rows = lax.all_gather(output_grad, 'expert', axis=0, tiled=True)]
    unnamed x27 -> x11, local copies, waits for them, and re-layouts: 60.9 us -> 2.93 us
    all_to_all x4 -> x0, starting transfers between devices: 53 us -> none  [the longest x1 19.7 us: on_device(): lax.all_to_all(to_slots(output_grad), 'expert', split_axis=0, concat_axis...]
    reshape x4 -> x0, local copies, waits for them, and re-layouts: 27.7 us -> none  [the longest x1 9.51 us: on_device(): grad_rows = recv_grads.reshape(slot_count, model_width)]
    all_to_all x5 -> x0, local copies, waits for them, and re-layouts: 25.1 us -> none  [the longest x2 8.5 us: on_device(): lax.all_to_all(to_slots(saved_inputs), 'expert', split_axis=0, concat_axi...]
  transfers between devices with their start and end apart: 6 -> 5, of which waited for: 4 -> 5; matrix products, arithmetic and copies ran while one was open for 36% -> 10% of each run, Pallas kernels for 0% -> 0%
where the time goes in v1:
time: 332 us
  waiting for transfers between devices  232 us (70%)
  matrix products  55.2 us (17%)
  blocking collectives  23.8 us (7%)
  between operations  13.9 us (4%)
    reduce_scatter x1, waiting for transfers between devices, dense_form(): lax.psum_scatter(part_rows, 'expert', scatter_dimension=0, tiled=True)  75 us
    all_gather x1, waiting for transfers between devices, dense_form(): grad_rows = lax.all_gather(output_grad, 'expert', axis=0, tiled=True)  53.9 us
    all_gather x1, waiting for transfers between devices, dense_form(): input_rows = lax.all_gather(saved_inputs, 'expert', axis=0, tiled=True)  46.7 us
    reduce_scatter x1, waiting for transfers between devices, dense_form(): lax.psum_scatter(jnp.concatenate([front, rear], axis=1).astype(jnp.bfloat...  41.6 us
    all_gather x1, blocking collectives, dense_form(): all_gates = lax.all_gather(gate_table, 'expert', axis=0, tiled=True)  23.8 us
    reduce_scatter x1, waiting for transfers between devices, dense_form(): lax.psum_scatter(own_rows, 'dp', scatter_dimension=1, tiled=True)  13.7 us
    dot_general x1, matrix products, dense_form(): lax.dot_general(grad_rows, down_w, contract_last, preferred_element_type=...  10.2 us
    dot_general x1, matrix products, dense_form(): pre_gate = jnp.dot(input_rows, gate_w, preferred_element_type=jnp.float32)  9.54 us
  transfers between devices with their start and end apart: 5, of which 5 were waited for; matrix products, arithmetic and copies ran while one was open for 10% of the time, Pallas kernels for 0%

profile of v1, /device:TPU:0, one launch (start us, length us, event | category | flops | bytes accessed | tf_op | source)
XLA Modules:
  0.0 331.8 jit_solution(12688891040194044894)
XLA Ops:
  7.2 0.0 copy-start
  7.2 0.0 all-gather.6.cloned.1.call-start
  7.2 0.7 all-gather.6.cloned.1.call-update
  7.9 0.0 all-gather.4.cloned.1.call-start
  8.0 0.7 all-gather.4.cloned.1.call-update
  8.7 0.0 reduce-scatter.4.cloned.1.call-start
  8.7 0.7 convert_element_type.32
  9.4 0.7 select_reduce_fusion.1
  10.1 23.8 %all-gather = bf16[16,64,16]{1,2,0:T(8,128)(2,1)S(1)} all-gather(bf16[1,64,16]{1,2,0:T(8,128)(2,1)S(1)} %bitcast.44), channel_id=1, replica_groups=mesh['dp'=2,'expert'=16] {'expert'}, dimensions={0}, use_global_device_ids=true | all-gather | bytes 34816 | tf_op jit(solution)/shard_map/all_gather | solution.py:122
  33.9 0.1 reshape.23
  34.1 0.1 select_reduce_fusion
  34.1 46.7 %all-gather.6.cloned.1.call-done = bf16[1024,3584]{1,0:T(8,128)(2,1)} async-done(((bf16[64,3584]{1,0:T(8,128)(2,1)}), bf16[1024,3584]{1,0:T(8,128)(2,1)}) %all-gather.6.cloned.1.call-update) | async-done | bytes 7340048 | tf_op jit(solution)/shard_map/all_gather | solution.py:123
  80.8 9.5 %fusion.4 = f32[1024,512]{1,0:T(8,128)} fusion(bf16[1024,3584]{1,0:T(8,128)(2,1)} %all-gather.6.cloned.1.call-done, bf16[1,3584,512]{2,1,0:T(8,128)(2,1)} %param.12), kind=kOutput, calls=%fused_computation.7 | convolution fusion | flops 3758096384 | bytes 13107200 | tf_op jit(solution)/shard_map/dot_general | solution.py:136
  90.4 5.3 %fusion.7 = f32[1024,512]{1,0:T(8,128)} fusion(bf16[1024,3584]{1,0:T(8,128)(2,1)S(1)} %copy-done.1, bf16[1,3584,512]{2,1,0:T(8,128)(2,1)S(1)} %copy-done.3), kind=kOutput, calls=%fused_computation.10 | convolution fusion | flops 3758096384 | bytes 13107200 | tf_op jit(solution)/shard_map/dot_general | solution.py:137
  95.6 53.9 %all-gather.4.cloned.1.call-done = bf16[1024,3584]{1,0:T(8,128)(2,1)} async-done(((bf16[64,3584]{1,0:T(8,128)(2,1)}), bf16[1024,3584]{1,0:T(8,128)(2,1)}) %all-gather.4.cloned.1.call-update) | async-done | bytes 7340048 | tf_op jit(solution)/shard_map/all_gather | solution.py:124
  149.5 10.2 %multiply_convert_fusion.1 = (bf16[1024,512]{1,0:T(8,128)(2,1)S(1)}, bf16[1024,512]{1,0:T(8,128)(2,1)S(1)}) fusion(f32[1024]{0:T(1024)S(1)} %select_reduce_fusion, f32[1024,512]{1,0:T(8,128)} %fusion.4, f32[1024,512]{1,0:T(8,128)} %fusion.7, bf16[1024,3584]{1,0:T(8,128)(2,1)} %all-gather.4.cloned.1.call-done, bf16[1,512,3584]{2,1,0:T(8,128)(2,1)} %param.14), kind=kOutput, calls=%fused_computation.16 | convolution fusion | flops 3765436416 | bytes 17305600 | tf_op jit(solution)/shard_map/dot_general | solution.py:138
  159.7 7.4 %fusion.2 = f32[1024,3584]{1,0:T(8,128)} fusion(bf16[1024,512]{1,0:T(8,128)(2,1)S(1)} %get-tuple-element.11, bf16[1,3584,512]{2,1,0:T(8,128)(2,1)S(1)} %copy-done.2), kind=kOutput, calls=%fused_computation.5 | convolution fusion | flops 3758096384 | bytes 19398656 | tf_op jit(solution)/shard_map/dot_general | solution.py:148
  167.2 9.4 %add_convert_fusion = bf16[1024,3584]{1,0:T(8,128)(2,1)} fusion(f32[1024,3584]{1,0:T(8,128)} %fusion.2, bf16[1024,512]{1,0:T(8,128)(2,1)S(1)} %get-tuple-element.10, bf16[1,3584,512]{2,1,0:T(8,128)(2,1)S(1)} %copy-done.4), kind=kOutput, calls=%fused_computation | convolution fusion | flops 3765436416 | bytes 26738688 | tf_op jit(solution)/shard_map/dot_general | solution.py:149
  176.5 0.0 reduce-scatter.4.cloned.1.call-update
  176.6 0.2 reduce-scatter.8.cloned.1.call-start
  176.8 0.5 convolution_convert_fusion.2
  177.3 0.5 convolution_convert_fusion.3
  177.8 5.2 %fusion = bf16[3584,256]{0,1:T(8,128)(2,1)S(1)} fusion(bf16[1024,3584]{1,0:T(8,128)(2,1)} %all-gather.6.cloned.1.call-done, bf16[1024,128]{0,1:T(8,128)(2,1)S(1)} %convolution_convert_fusion.2, bf16[1024,128]{0,1:T(8,128)(2,1)S(1)} %convolution_convert_fusion.3), kind=kOutput, calls=%fused_computation.2 | convolution fusion | flops 1881014272 | bytes 9699328 | tf_op jit(solution)/shard_map/dot_general | solution.py:159
  182.9 7.3 %fusion.1 = bf16[3584,128]{0,1:T(8,128)(2,1)S(1)} fusion(bf16[1024,3584]{1,0:T(8,128)(2,1)} %all-gather.4.cloned.1.call-done, f32[1024,512]{1,0:T(8,128)} %fusion.7, f32[1024,512]{1,0:T(8,128)} %fusion.4, f32[1024]{0:T(1024)S(1)} %select_reduce_fusion, bf16[1,512,128]{2,1,0:T(8,128)(2,1)S(1)} %copy-done), kind=kOutput, calls=%fused_computation.4 | convolution fusion | flops 1077608448 | bytes 12587008 | tf_op jit(solution)/shard_map/dot_general | solution.py:162
  190.3 1.7 pad_maximum_fusion
  192.0 0.0 reduce-scatter.8.cloned.1.call-update
  192.0 0.0 reduce-scatter.6.cloned.1.call-start
  192.1 75.0 %reduce-scatter.4.cloned.1.call-done = bf16[64,3584]{1,0:T(8,128)(2,1)} async-done(((bf16[1024,3584]{1,0:T(8,128)(2,1)}), bf16[64,3584]{1,0:T(8,128)(2,1)}) %reduce-scatter.4.cloned.1.call-update) | async-done | bytes 458768 | tf_op jit(solution)/shard_map/reduce_scatter | solution.py:151
  267.1 0.0 reduce-scatter.6.cloned.1.call-update
  267.1 41.6 %reduce-scatter.8.cloned.1.call-done = bf16[1792,384]{0,1:T(8,128)(2,1)} async-done(((bf16[3584,384]{0,1:T(8,128)(2,1)}), bf16[1792,384]{0,1:T(8,128)(2,1)}) %reduce-scatter.8.cloned.1.call-update) | async-done | bytes 1376272 | tf_op jit(solution)/shard_map/reduce_scatter | solution.py:163
  308.7 2.9 copy.21
  311.6 13.7 %reduce-scatter.6.cloned.1.call-done = bf16[64,1792]{1,0:T(8,128)(2,1)} async-done(((bf16[64,3584]{1,0:T(8,128)(2,1)}), bf16[64,1792]{1,0:T(8,128)(2,1)}) %reduce-scatter.6.cloned.1.call-update) | async-done | bytes 229392 | tf_op jit(solution)/shard_map/reduce_scatter | solution.py:152
  (11 shorter events, 0.0 us)
Async XLA Ops:
  7.2 169.6 %copy-start = (bf16[1,512,128]{2,1,0:T(8,128)(2,1)S(1)}, bf16[1,512,128]{2,1,0:T(8,128)(2,1)}, u32[]{:S(2)}) copy-start(bf16[1,512,128]{2,1,0:T(8,128)(2,1)} %param.15) | copy-start | bytes 393220
  7.2 73.6 %all-gather.6.cloned.1.call-start = ((), (), s32[]{:S(2)}) async-start(), calls=%async_computation.4 | async-start | bytes 7798784 | tf_op jit(solution)/shard_map/all_gather | solution.py:123
  7.9 141.6 %all-gather.4.cloned.1.call-start = ((), (), s32[]{:S(2)}) async-start(), calls=%async_computation.3 | async-start | bytes 7798784 | tf_op jit(solution)/shard_map/all_gather | solution.py:124
  8.7 258.4 %reduce-scatter.4.cloned.1.call-start = ((), (), s32[]{:S(2)}) async-start(), calls=%async_computation.5 | async-start | bytes 7798784 | tf_op jit(solution)/shard_map/reduce_scatter | solution.py:151
  80.8 9.5 %copy-start.1 = (bf16[1024,3584]{1,0:T(8,128)(2,1)S(1)}, bf16[1024,3584]{1,0:T(8,128)(2,1)}, u32[]{:S(2)}) copy-start(bf16[1024,3584]{1,0:T(8,128)(2,1)} %all-gather.6.cloned.1.call-done) | copy-start | bytes 22020100
  80.8 9.5 %copy-start.3 = (bf16[1,3584,512]{2,1,0:T(8,128)(2,1)S(1)}, bf16[1,3584,512]{2,1,0:T(8,128)(2,1)}, u32[]{:S(2)}) copy-start(bf16[1,3584,512]{2,1,0:T(8,128)(2,1)} %param.13) | copy-start | bytes 11010052
  149.5 10.2 %copy-start.2 = (bf16[1,3584,512]{2,1,0:T(8,128)(2,1)S(1)}, bf16[1,3584,512]{2,1,0:T(8,128)(2,1)}, u32[]{:S(2)}) copy-start(bf16[1,3584,512]{2,1,0:T(8,128)(2,1)} %param.12) | copy-start | bytes 11010052
  159.7 7.4 %copy-start.4 = (bf16[1,3584,512]{2,1,0:T(8,128)(2,1)S(1)}, bf16[1,3584,512]{2,1,0:T(8,128)(2,1)}, u32[]{:S(2)}) copy-start(bf16[1,3584,512]{2,1,0:T(8,128)(2,1)} %param.13) | copy-start | bytes 11010052
  176.6 132.1 %reduce-scatter.8.cloned.1.call-start = ((), (), s32[]{:S(2)}) async-start(), calls=%async_computation.7 | async-start | bytes 4128768 | tf_op jit(solution)/shard_map/reduce_scatter | solution.py:163
  192.0 133.3 %reduce-scatter.6.cloned.1.call-start = ((), (), s32[]{:S(2)}) async-start(), calls=%async_computation.6 | async-start | bytes 688128 | tf_op jit(solution)/shard_map/reduce_scatter | solution.py:152
Sparse Core Ops, SparseCore 0:
  10.3 70.4 all-gather.5
  83.1 66.4 all-gather.3
  176.7 90.3 reduce-scatter.3
  269.8 38.8 reduce-scatter.7
  311.4 13.9 reduce-scatter.5

commit v2 on v1

--- a/solution.py
+++ b/solution.py
@@ -1,6 +1,10 @@
+import functools
+
 import jax
 import jax.numpy as jnp
 from jax import lax
+from jax.experimental import pallas as pl
+from jax.experimental.pallas import tpu as pltpu
 from jax.sharding import PartitionSpec as P
 
 
@@ -106,22 +110,218 @@
     )
     return (token_grad, projected)
 
+MESH = pl.DeviceIdType.MESH
+LANES = 128
+
+
+def gather_kernel(
+    depth, split, x_in, y_in, g_in, x_all, y_all, g_all,
+    x_hold, y_hold, g_hold, recv_sem, up_sem, down_sem, side_sem, plane_sem, core_sem, local_sem,
+):
+    dp = lax.axis_index("dp")
+    me = lax.axis_index("expert")
+    z, y, core = me // 4, (me // 2) % 2, me % 2
+    rows, width = x_in.shape
+    own_cols = pl.ds(pl.multiple_of(dp * split, LANES), split)
+    far_cols = pl.ds(pl.multiple_of((1 - dp) * split, LANES), split)
+    rest_cols = pl.ds(2 * split, width - 2 * split)
+    all_cols = pl.ds(0, g_in.shape[1])
+    pieces = (
+        (x_in, x_all, own_cols), (y_in, y_all, own_cols),
+        (x_in, x_all, rest_cols), (y_in, y_all, rest_cols),
+        (g_in, g_all, all_cols),
+        (x_in, x_all, far_cols), (y_in, y_all, far_cols),
+    )
+    planar = range(5)
+
+    def index(zz, yy, cc):
+        return zz * 4 + yy * 2 + cc
+
+    def landed(piece, item):
+        _, whole, cols = pieces[piece]
+        return whole.at[pl.ds(pl.multiple_of(item * rows, rows), rows), cols]
+
+    def copy(piece, item, own, sem, device, recv_piece):
+        start, _, cols = pieces[piece]
+        src = start.at[:, cols] if own else landed(piece, item)
+        return pltpu.make_async_remote_copy(
+            src_ref=src,
+            dst_ref=landed(piece, item),
+            send_sem=sem,
+            recv_sem=recv_sem.at[recv_piece, item],
+            device_id=device,
+            device_id_type=MESH,
+        )
+
+    def up(piece, zz, own=False):
+        return copy(piece, index(zz, y, core), own, up_sem.at[piece, zz], (dp, me + 4), piece)
+
+    def down(piece, zz, own=False):
+        return copy(piece, index(zz, y, core), own, down_sem.at[piece, zz], (dp, me - 4), piece)
+
+    def side(piece, zz, own=False):
+        partner = index(z, 1 - y, core)
+        return copy(piece, index(zz, y, core), own, side_sem.at[piece, zz], (dp, partner), piece)
+
+    def plane(piece, zz, yy):
+        item = index(zz, yy, core)
+        return copy(piece, item, False, plane_sem.at[piece, item // 2], (1 - dp, me), piece + 5)
+
+    def other(piece, zz, yy, own=False):
+        item = index(zz, yy, core)
+        partner = index(z, y, 1 - core)
+        return copy(piece, item, own, core_sem.at[piece, item // 2], (dp, partner), piece)
+
+    def arrive(piece, item):
+        copy(piece, item, False, core_sem.at[0, 0], (dp, me), piece).wait_recv()
+
+    barrier = pltpu.get_barrier_semaphore()
+
+    def greet(device):
+        pl.semaphore_signal(barrier, inc=1, device_id=device, device_id_type=MESH)
+
+    greet((1 - dp, me))
+    greet((dp, index(z, 1 - y, core)))
+    greet((dp, index(z, y, 1 - core)))
+    pl.when(z > 0)(lambda: greet((dp, me - 4)))
+    pl.when(z < depth - 1)(lambda: greet((dp, me + 4)))
+    pl.semaphore_wait(barrier, 3 + jnp.minimum(z, 1) + jnp.minimum(depth - 1 - z, 1))
+
+    for piece in planar:
+        pl.when(z < depth - 1)(lambda piece=piece: up(piece, z, True).start())
+        pl.when(z > 0)(lambda piece=piece: down(piece, z, True).start())
+        side(piece, z, True).start()
+    for piece in range(7):
+        other(piece, z, y, True).start()
+    mine = pl.ds(pl.multiple_of(me * rows, rows), rows)
+    holds = ((x_in, x_hold, x_all), (y_in, y_hold, y_all), (g_in, g_hold, g_all))
+    into = [pltpu.make_async_copy(a, b, local_sem.at[i]) for i, (a, b, _) in enumerate(holds)]
+    out = [
+        pltpu.make_async_copy(b, c.at[mine], local_sem.at[3 + i])
+        for i, (_, b, c) in enumerate(holds)
+    ]
+    for one in into:
+        one.start()
+    for one, two in zip(into, out):
+        one.wait()
+        two.start()
+
+    def spots(away):
+        if away == 0:
+            return [(z, None)]
+        return [(z - away, z >= away), (z + away, z + away < depth)]
+
+    def guarded(condition, act):
+        act() if condition is None else pl.when(condition)(act)
+
+    def along_z(piece, zz, from_below):
+        def act():
+            arrive(piece, index(zz, y, core))
+            if from_below:
+                pl.when(z < depth - 1)(lambda: up(piece, zz).start())
+            else:
+                pl.when(z > 0)(lambda: down(piece, zz).start())
+            side(piece, zz).start()
+            if piece < 2:
+                plane(piece, zz, y).start()
+            other(piece, zz, y).start()
+        return act
+
+    def from_side(piece, zz):
+        def act():
+            arrive(piece, index(zz, 1 - y, core))
+            if piece < 2:
+                plane(piece, zz, 1 - y).start()
+            other(piece, zz, 1 - y).start()
+        return act
+
+    def from_plane(piece, zz, yy):
+        def act():
+            arrive(piece, index(zz, yy, core))
+            other(piece, zz, yy).start()
+        return act
+
+    for step in range(1, depth + 2):
+        for piece in planar:
+            if step < depth:
+                for below, (zz, there) in zip((True, False), spots(step)):
+                    guarded(there, along_z(piece, zz, below))
+            if step <= depth:
+                for zz, there in spots(step - 1):
+                    guarded(there, from_side(piece, zz))
+        for piece in (5, 6):
+            if 1 <= step - 1 < depth:
+                for zz, there in spots(step - 1):
+                    guarded(there, from_plane(piece, zz, y))
+            if step >= 2:
+                for zz, there in spots(step - 2):
+                    guarded(there, from_plane(piece, zz, 1 - y))
+
+    for piece in range(7):
+        for pair in range(2 * depth):
+            arrive(piece, pair * 2 + 1 - core)
+    for piece in planar:
+        for zz in range(depth):
+            pl.when((zz <= z) & (z < depth - 1))(lambda p=piece, q=zz: up(p, q).wait_send())
+            pl.when((zz >= z) & (z > 0))(lambda p=piece, q=zz: down(p, q).wait_send())
+            side(piece, zz).wait_send()
+    for piece in range(2):
+        for pair in range(2 * depth):
+            pl.when(pair != me // 2)(
+                lambda p=piece, q=pair: plane(p, q // 2, q % 2).wait_send()
+            )
+    for piece in range(7):
+        for pair in range(2 * depth):
+            other(piece, pair // 2, pair % 2).wait_send()
+    for one in out:
+        one.wait()
+
+
+def gather_rows(saved_inputs, output_grad, gate_table):
+    expert_count = lax.axis_size("expert")
+    rows, width = saved_inputs.shape
+    depth = expert_count // 4
+    split = width * 5 // 14 // LANES * LANES
+    gate_width = gate_table.shape[1]
+    dma = pltpu.SemaphoreType.DMA
+    whole = pl.BlockSpec(memory_space=pl.ANY)
+    return pl.pallas_call(
+        functools.partial(gather_kernel, depth, split),
+        out_shape=[
+            jax.ShapeDtypeStruct((expert_count * rows, width), jnp.bfloat16),
+            jax.ShapeDtypeStruct((expert_count * rows, width), jnp.bfloat16),
+            jax.ShapeDtypeStruct((expert_count * rows, gate_width), jnp.bfloat16),
+        ],
+        in_specs=[whole] * 3,
+        out_specs=[whole] * 3,
+        scratch_shapes=[
+            pltpu.VMEM((rows, width), jnp.bfloat16),
+            pltpu.VMEM((rows, width), jnp.bfloat16),
+            pltpu.VMEM((rows, gate_width), jnp.bfloat16),
+            dma((7, expert_count)),
+            dma((5, depth)),
+            dma((5, depth)),
+            dma((5, depth)),
+            dma((2, 2 * depth)),
+            dma((7, 2 * depth)),
+            dma((6,)),
+        ],
+        compiler_params=pltpu.CompilerParams(collective_id=0, has_side_effects=True),
+    )(saved_inputs, output_grad, gate_table)
+
 
 def dense_form(
     saved_inputs, output_grad, routes, route_gates, expert_gate, expert_up, expert_down, proj_basis
 ):
     model_width = saved_inputs.shape[1]
-    expert_count = lax.axis_size("expert")
     group_count = lax.axis_size("dp")
     column_width = model_width // group_count
-    experts = jnp.arange(expert_count, dtype=jnp.int32)
+    experts = jnp.arange(LANES, dtype=jnp.int32)
     chosen = routes[:, :, None] == experts[None, None, :]
     gate_table = jnp.sum(
         jnp.where(chosen, route_gates.astype(jnp.float32)[:, :, None], 0.0), axis=1
     ).astype(jnp.bfloat16)
-    all_gates = lax.all_gather(gate_table, "expert", axis=0, tiled=True)
-    input_rows = lax.all_gather(saved_inputs, "expert", axis=0, tiled=True)
-    grad_rows = lax.all_gather(output_grad, "expert", axis=0, tiled=True)
+    input_rows, grad_rows, all_gates = gather_rows(saved_inputs, output_grad, gate_table)
     own = experts == lax.axis_index("expert")
     gain = jnp.sum(
         jnp.where(own[None, :], all_gates.astype(jnp.float32), 0.0), axis=1, keepdims=True

time: 332 us -> 268 us (0.81)
  waiting for transfers between devices: 232 us -> 131 us
  Pallas kernels: 0 us -> 63.3 us
  blocking collectives: 23.8 us -> 0 us
  matrix products: 55.2 us -> 51.2 us
    all_gather x2 -> x0, waiting for transfers between devices: 101 us -> none  [the longest x1 53.9 us: dense_form(): grad_rows = lax.all_gather(output_grad, 'expert', axis=0, tiled=True)]
    pallas_call x0 -> x1, Pallas kernels: none -> 63.3 us  [gather_rows(): pl.pallas_call(functools.partial(gather_kernel, depth, split), out_shape=...]
    all_gather x1 -> x0, blocking collectives: 23.8 us -> none  [dense_form(): all_gates = lax.all_gather(gate_table, 'expert', axis=0, tiled=True)]
    dot_general x1, matrix products: 10.2 us -> 6.3 us  [dense_form(): lax.dot_general(grad_rows, down_w, contract_last, preferred_element_type=...]
  transfers between devices with their start and end apart: 5 -> 3, of which waited for: 5 -> 3; matrix products, arithmetic and copies ran while one was open for 10% -> 7% of each run, Pallas kernels for 0% -> 0%
where the time goes in v2:
time: 268 us; the launch traced here: 267 us
  waiting for transfers between devices  131 us (49%)
  Pallas kernels  63.3 us (24%)
  matrix products  51.2 us (19%)
  between operations  13.9 us (5%)
  local copies, waits for them, and re-layouts  4.48 us (2%)
  other arithmetic  2.69 us (1%)
    reduce_scatter x1, waiting for transfers between devices, dense_form(): lax.psum_scatter(part_rows, 'expert', scatter_dimension=0, tiled=True)  75.7 us
    pallas_call x1, Pallas kernels, gather_rows(): pl.pallas_call(functools.partial(gather_kernel, depth, split), out_shape=...  63.3 us
    reduce_scatter x1, waiting for transfers between devices, dense_form(): lax.psum_scatter(jnp.concatenate([front, rear], axis=1).astype(jnp.bfloat...  41.7 us
    reduce_scatter x1, waiting for transfers between devices, dense_form(): lax.psum_scatter(own_rows, 'dp', scatter_dimension=1, tiled=True)  13.9 us
    dot_general x1, matrix products, dense_form(): pre_gate = jnp.dot(input_rows, gate_w, preferred_element_type=jnp.float32)  9.54 us
    dot_general x1, matrix products, dense_form(): lax.dot_general(grad_up, up_w, contract_last, preferred_element_type=jnp....  9.36 us
    dot_general x1, matrix products, dense_form(): lax.dot_general(grad_gate, gate_w, contract_last, preferred_element_type=...  7.42 us
    dot_general x1, matrix products, dense_form(): lax.dot_general(grad_rows, coef_down, contract_first, preferred_element_t...  7.26 us
  transfers between devices with their start and end apart: 3, of which 3 were waited for; matrix products, arithmetic and copies ran while one was open for 7% of the time, Pallas kernels for 0%

profile of v2, /device:TPU:0, one launch (start us, length us, event | category | flops | bytes accessed | tf_op | source)
XLA Modules:
  0.0 267.3 jit_solution(9831368737263059601)
XLA Ops:
  7.2 0.0 copy-start
  7.2 0.0 reduce-scatter.4.cloned.1.call-start
  7.2 0.8 copy.13
  8.0 0.8 copy.14
  8.8 0.8 select_reduce_fusion.1.g_in
  9.6 63.3 %shard_map.95 = (bf16[1024,3584]{1,0:T(8,128)(2,1)}, bf16[1024,3584]{1,0:T(8,128)(2,1)}, bf16[1024,128]{1,0:T(8,128)(2,1)}) custom-call(bf16[64,3584]{1,0:T(8,128)(2,1)} %x_in.1, bf16[64,3584]{1,0:T(8,128)(2,1)} %y_in.1, bf16[64,128]{1,0:T(8,128)(2,1)} %select_reduce_fusion.1.g_in), custom_call_target="tpu_custom_call" | custom-call | tf_op jit(solution)/shard_map/pallas_call | solution.py:288
  72.9 0.0 copy-start.2
  73.0 0.0 copy-start.5
  73.0 0.0 slice-start
  73.0 9.5 %fusion.2 = f32[1024,512]{1,0:T(8,128)} fusion(bf16[1024,3584]{1,0:T(8,128)(2,1)} %get-tuple-element.7, bf16[1,3584,512]{2,1,0:T(8,128)(2,1)} %param.12), kind=kOutput, calls=%fused_computation.5 | convolution fusion | flops 3758096384 | bytes 13107200 | tf_op jit(solution)/shard_map/dot_general | solution.py:336
  82.5 0.0 slice-start.1
  82.5 0.0 copy-start.3
  82.6 5.3 %fusion.5 = f32[1024,512]{1,0:T(8,128)} fusion(bf16[1024,3584]{1,0:T(8,128)(2,1)S(1)} %copy-done.2, bf16[1,3584,512]{2,1,0:T(8,128)(2,1)S(1)} %copy-done.5), kind=kOutput, calls=%fused_computation.8 | convolution fusion | flops 3758096384 | bytes 13107200 | tf_op jit(solution)/shard_map/dot_general | solution.py:337
  87.8 0.1 select_reduce_fusion
  88.0 0.0 copy-start.4
  88.0 6.3 %multiply_convert_fusion.1 = (bf16[1024,512]{1,0:T(8,128)(2,1)S(1)}, bf16[1024,512]{1,0:T(8,128)(2,1)S(1)}) fusion(f32[1024]{0:T(1024)S(1)} %select_reduce_fusion, f32[1024,512]{1,0:T(8,128)} %fusion.2, f32[1024,512]{1,0:T(8,128)} %fusion.5, bf16[1024,3584]{1,0:T(8,128)(2,1)S(1)} %bitcast.36, bf16[1,512,3584]{2,1,0:T(8,128)(2,1)S(1)} %copy-done.3), kind=kOutput, calls=%fused_computation.14 | convolution fusion | flops 3765436416 | bytes 17305600 | tf_op jit(solution)/shard_map/dot_general | solution.py:338
  94.4 7.4 %fusion = f32[1024,3584]{1,0:T(8,128)} fusion(bf16[1024,512]{1,0:T(8,128)(2,1)S(1)} %get-tuple-element.13, bf16[1,3584,512]{2,1,0:T(8,128)(2,1)S(1)} %copy-done.4), kind=kOutput, calls=%fused_computation.3 | convolution fusion | flops 3758096384 | bytes 19398656 | tf_op jit(solution)/shard_map/dot_general | solution.py:348
  101.8 9.4 %add_convert_fusion = bf16[1024,3584]{1,0:T(8,128)(2,1)} fusion(f32[1024,3584]{1,0:T(8,128)} %fusion, bf16[1024,512]{1,0:T(8,128)(2,1)S(1)} %get-tuple-element.12, bf16[1,3584,512]{2,1,0:T(8,128)(2,1)S(1)} %copy-done.5), kind=kOutput, calls=%fused_computation | convolution fusion | flops 3765436416 | bytes 26738688 | tf_op jit(solution)/shard_map/dot_general | solution.py:349
  111.1 0.0 reduce-scatter.4.cloned.1.call-update
  111.2 0.2 reduce-scatter.8.cloned.1.call-start
  111.4 0.4 convolution_convert_fusion.2
  111.8 0.4 convolution_convert_fusion.3
  112.3 5.2 %convolution_convert_fusion = bf16[3584,256]{0,1:T(8,128)(2,1)S(1)} fusion(bf16[1024,3584]{1,0:T(8,128)(2,1)} %get-tuple-element.7, bf16[1024,128]{1,0:T(8,128)(2,1)S(1)} %convolution_convert_fusion.2, bf16[1024,128]{1,0:T(8,128)(2,1)S(1)} %convolution_convert_fusion.3), kind=kOutput, calls=%fused_computation.1 | convolution fusion | flops 1881014272 | bytes 9699328 | tf_op jit(solution)/shard_map/dot_general | solution.py:359
  117.5 7.3 %convolution_convert_fusion.1 = bf16[3584,128]{0,1:T(8,128)(2,1)S(1)} fusion(bf16[1024,3584]{1,0:T(8,128)(2,1)} %get-tuple-element.6, f32[1024,512]{1,0:T(8,128)} %fusion.5, f32[1024,512]{1,0:T(8,128)} %fusion.2, f32[1024]{0:T(1024)S(1)} %select_reduce_fusion, bf16[1,512,128]{2,1,0:T(8,128)(2,1)S(1)} %copy-done), kind=kOutput, calls=%fused_computation.2 | convolution fusion | flops 1077608448 | bytes 12587008 | tf_op jit(solution)/shard_map/dot_general | solution.py:362
  124.7 1.7 pad_maximum_fusion
  126.5 0.0 reduce-scatter.8.cloned.1.call-update
  126.5 0.0 reduce-scatter.6.cloned.1.call-start
  126.5 75.7 %reduce-scatter.4.cloned.1.call-done = bf16[64,3584]{1,0:T(8,128)(2,1)} async-done(((bf16[1024,3584]{1,0:T(8,128)(2,1)}), bf16[64,3584]{1,0:T(8,128)(2,1)}) %reduce-scatter.4.cloned.1.call-update) | async-done | bytes 458768 | tf_op jit(solution)/shard_map/reduce_scatter | solution.py:351
  202.3 0.0 reduce-scatter.6.cloned.1.call-update
  202.3 41.7 %reduce-scatter.8.cloned.1.call-done = bf16[1792,384]{0,1:T(8,128)(2,1)} async-done(((bf16[3584,384]{0,1:T(8,128)(2,1)}), bf16[1792,384]{0,1:T(8,128)(2,1)}) %reduce-scatter.8.cloned.1.call-update) | async-done | bytes 1376272 | tf_op jit(solution)/shard_map/reduce_scatter | solution.py:363
  244.0 2.9 %copy.15 = f32[1,1792,3,128]{3,1,2,0:T(8,128)} copy(bf16[1,1792,3,128]{1,3,2,0:T(8,128)(2,1)} %bitcast.34) | data formatting | bytes 4128768
  246.9 13.9 %reduce-scatter.6.cloned.1.call-done = bf16[64,1792]{1,0:T(8,128)(2,1)} async-done(((bf16[64,3584]{1,0:T(8,128)(2,1)}), bf16[64,1792]{1,0:T(8,128)(2,1)}) %reduce-scatter.6.cloned.1.call-update) | async-done | bytes 229392 | tf_op jit(solution)/shard_map/reduce_scatter | solution.py:352
  (11 shorter events, 0.0 us)
Async XLA Ops:
  7.2 104.2 %copy-start = (bf16[1,512,128]{2,1,0:T(8,128)(2,1)S(1)}, bf16[1,512,128]{2,1,0:T(8,128)(2,1)}, u32[]{:S(2)}) copy-start(bf16[1,512,128]{2,1,0:T(8,128)(2,1)} %param.15) | copy-start | bytes 393220
  7.2 195.1 %reduce-scatter.4.cloned.1.call-start = ((), (), s32[]{:S(2)}) async-start(), calls=%async_computation.3 | async-start | bytes 7798784 | tf_op jit(solution)/shard_map/reduce_scatter | solution.py:351
  72.9 9.6 %copy-start.2 = (bf16[1024,3584]{1,0:T(8,128)(2,1)S(1)}, bf16[1024,3584]{1,0:T(8,128)(2,1)}, u32[]{:S(2)}) copy-start(bf16[1024,3584]{1,0:T(8,128)(2,1)} %get-tuple-element.7) | copy-start | bytes 22020100
  73.0 9.6 %copy-start.5 = (bf16[1,3584,512]{2,1,0:T(8,128)(2,1)S(1)}, bf16[1,3584,512]{2,1,0:T(8,128)(2,1)}, u32[]{:S(2)}) copy-start(bf16[1,3584,512]{2,1,0:T(8,128)(2,1)} %param.13) | copy-start | bytes 11010052
  73.0 15.0 %slice-start = ((s8[7340032]{0:T(1024)(128)(4,1)}), s8[4194304]{0:T(1024)(128)(4,1)S(1)}, s32[]{:S(2)}) async-start(s8[7340032]{0:T(1024)(128)(4,1)} %bitcast.35), calls=%async_computation.6 | async-start | bytes 8388608
  82.5 5.3 %copy-start.1 = (bf16[1024,128]{1,0:T(8,128)(2,1)S(1)}, bf16[1024,128]{1,0:T(8,128)(2,1)}, u32[]{:S(2)}) copy-start(bf16[1024,128]{1,0:T(8,128)(2,1)} %get-tuple-element.5) | copy-start | bytes 786436
  82.5 5.5 %slice-start.1 = ((s8[7340032]{0:T(1024)(128)(4,1)}), s8[3145728]{0:T(1024)(128)(4,1)S(1)}, s32[]{:S(2)}) async-start(s8[7340032]{0:T(1024)(128)(4,1)} %bitcast.35), calls=%async_computation.7 | async-start | bytes 6291456
  82.5 5.5 %copy-start.3 = (bf16[1,512,3584]{2,1,0:T(8,128)(2,1)S(1)}, bf16[1,512,3584]{2,1,0:T(8,128)(2,1)}, u32[]{:S(2)}) copy-start(bf16[1,512,3584]{2,1,0:T(8,128)(2,1)} %param.14) | copy-start | bytes 11010052
  88.0 6.3 %copy-start.4 = (bf16[1,3584,512]{2,1,0:T(8,128)(2,1)S(1)}, bf16[1,3584,512]{2,1,0:T(8,128)(2,1)}, u32[]{:S(2)}) copy-start(bf16[1,3584,512]{2,1,0:T(8,128)(2,1)} %param.12) | copy-start | bytes 11010052
  111.2 132.8 %reduce-scatter.8.cloned.1.call-start = ((), (), s32[]{:S(2)}) async-start(), calls=%async_computation.5 | async-start | bytes 4128768 | tf_op jit(solution)/shard_map/reduce_scatter | solution.py:363
  126.5 134.3 %reduce-scatter.6.cloned.1.call-start = ((), (), s32[]{:S(2)}) async-start(), calls=%async_computation.4 | async-start | bytes 688128 | tf_op jit(solution)/shard_map/reduce_scatter | solution.py:352
Sparse Core Ops, SparseCore 0:
  111.3 90.9 reduce-scatter.3
  205.1 38.8 reduce-scatter.7
  246.8 13.9 reduce-scatter.5

commit v3 on v2

--- a/solution.py
+++ b/solution.py
@@ -310,12 +310,223 @@
     )(saved_inputs, output_grad, gate_table)
 
 
+def scatter_kernel(
+    depth, part, terms, grad_out, proj_out,
+    mine, from_core, from_side, from_below, from_above, final, from_plane, own_terms, far_terms,
+    local_sem, core_sem, side_sem, up_sem, down_sem, plane_sem, terms_sem,
+):
+    dp = lax.axis_index("dp")
+    me = lax.axis_index("expert")
+    z, y, core = me // 4, (me // 2) % 2, me % 2
+    pairs = 2 * depth
+    width = part.shape[3]
+    chunk = width // 4
+    order = (0, 2, 1, 3)
+    core_device = (dp, z * 4 + y * 2 + 1 - core)
+    side_device = (dp, z * 4 + (1 - y) * 2 + core)
+    plane_device = (1 - dp, me)
+
+    def cols(k):
+        return pl.ds(k * chunk, chunk)
+
+    def remote(src, dst, sems, device):
+        return pltpu.make_async_remote_copy(
+            src_ref=src, dst_ref=dst, send_sem=sems[0], recv_sem=sems[1],
+            device_id=device, device_id_type=MESH,
+        )
+
+    def both(sem, *at):
+        return sem.at[(0,) + at], sem.at[(1,) + at]
+
+    def local_copy(k):
+        return pltpu.make_async_copy(
+            part.at[:, core, :, cols(k)], mine.at[:, :, cols(k)], local_sem.at[k]
+        )
+
+    def core_copy(k):
+        return remote(
+            part.at[:, 1 - core, :, cols(k)], from_core.at[:, :, cols(k)],
+            both(core_sem, k), core_device,
+        )
+
+    def side_copy(k, zz):
+        return remote(
+            mine.at[zz * 2 + 1 - y, :, cols(k)], from_side.at[zz, :, cols(k)],
+            both(side_sem, k, zz), side_device,
+        )
+
+    def up_copy(k, zz):
+        return remote(
+            mine.at[zz * 2 + y, :, cols(k)], from_below.at[zz, :, cols(k)],
+            both(up_sem, k, zz), (dp, me + 4),
+        )
+
+    def down_copy(k, zz):
+        return remote(
+            mine.at[zz * 2 + y, :, cols(k)], from_above.at[zz, :, cols(k)],
+            both(down_sem, k, zz), (dp, me - 4),
+        )
+
+    def plane_copy(k):
+        return remote(
+            final.at[:, cols(k)], from_plane.at[:, cols(k % 2)],
+            both(plane_sem, k % 2), plane_device,
+        )
+
+    terms_copy = remote(terms.at[1 - dp], far_terms, both(terms_sem), plane_device)
+    terms_local = pltpu.make_async_copy(terms.at[dp], own_terms, local_sem.at[4])
+
+    barrier = pltpu.get_barrier_semaphore()
+
+    def greet(device):
+        pl.semaphore_signal(barrier, inc=1, device_id=device, device_id_type=MESH)
+
+    greet(plane_device)
+    greet(side_device)
+    greet(core_device)
+    pl.when(z > 0)(lambda: greet((dp, me - 4)))
+    pl.when(z < depth - 1)(lambda: greet((dp, me + 4)))
+    pl.semaphore_wait(barrier, 3 + jnp.minimum(z, 1) + jnp.minimum(depth - 1 - z, 1))
+
+    for k in order:
+        core_copy(k).start()
+        local_copy(k).start()
+    terms_copy.start()
+    terms_local.start()
+
+    def add_into(slot, k, other):
+        total = mine[slot, :, cols(k)].astype(jnp.float32) + other.astype(jnp.float32)
+        mine[slot, :, cols(k)] = total.astype(jnp.bfloat16)
+
+    def over_cores(k):
+        local_copy(k).wait()
+        core_copy(k).wait_recv()
+        for zz in range(depth):
+            slot = zz * 2 + 1 - y
+            add_into(slot, k, from_core[slot, :, cols(k)])
+            side_copy(k, zz).start()
+        for zz in range(depth):
+            slot = zz * 2 + y
+            add_into(slot, k, from_core[slot, :, cols(k)])
+
+    def over_side(k):
+        for zz in reversed(range(depth)):
+            side_copy(k, zz).wait_recv()
+            add_into(zz * 2 + y, k, from_side[zz, :, cols(k)])
+            if zz > 0:
+                pl.when(z == 0)(lambda zz=zz: up_copy(k, zz).start())
+        for zz in range(depth - 1):
+            pl.when(z == depth - 1)(lambda zz=zz: down_copy(k, zz).start())
+
+    def along_z(k):
+        for far in reversed(range(1, depth)):
+            def rise(zz=far):
+                up_copy(k, zz).wait_recv()
+                add_into(zz * 2 + y, k, from_below[zz, :, cols(k)])
+                up_copy(k, zz).start()
+
+            def fall(zz=depth - 1 - far):
+                down_copy(k, zz).wait_recv()
+                add_into(zz * 2 + y, k, from_above[zz, :, cols(k)])
+                down_copy(k, zz).start()
+
+            pl.when((z > 0) & (z < far))(rise)
+            pl.when((z < depth - 1) & (z > depth - 1 - far))(fall)
+
+    def finish(k):
+        slot = z * 2 + y
+
+        def take_below():
+            up_copy(k, z).wait_recv()
+            add_into(slot, k, from_below[z, :, cols(k)])
+
+        def take_above():
+            down_copy(k, z).wait_recv()
+            add_into(slot, k, from_above[z, :, cols(k)])
+
+        pl.when(z > 0)(take_below)
+        pl.when(z < depth - 1)(take_above)
+        final[:, cols(k)] = mine[slot, :, cols(k)]
+        pl.when(dp != k // 2)(lambda: plane_copy(k).start())
+
+    stages = (over_cores, over_side, along_z, finish)
+    for step in range(len(order) + len(stages) - 1):
+        for number, stage in enumerate(stages):
+            if 0 <= step - number < len(order):
+                stage(order[step - number])
+
+    terms_local.wait()
+    terms_copy.wait()
+    rank = proj_out.shape[2]
+    for j in range(proj_out.shape[0]):
+        at = pl.ds(j * rank, rank)
+        proj_out[j] = own_terms[:, at].astype(jnp.float32) + far_terms[:, at].astype(jnp.float32)
+
+    for k in range(4):
+        def take_plane(k=k):
+            plane_copy(k).wait_recv()
+            total = final[:, cols(k)].astype(jnp.float32) + from_plane[:, cols(k % 2)].astype(
+                jnp.float32
+            )
+            grad_out[:, cols(k % 2)] = total.astype(jnp.bfloat16)
+
+        pl.when(dp == k // 2)(take_plane)
+        pl.when(dp != k // 2)(lambda k=k: plane_copy(k).wait_send())
+        core_copy(k).wait_send()
+        for zz in range(depth):
+            side_copy(k, zz).wait_send()
+            pl.when(zz > z)(lambda k=k, zz=zz: up_copy(k, zz).wait_send())
+            pl.when(zz < z)(lambda k=k, zz=zz: down_copy(k, zz).wait_send())
+
+
+def scatter_sums(part_rows, terms, rank_width):
+    group_count = lax.axis_size("dp")
+    expert_count = lax.axis_size("expert")
+    all_rows, width = part_rows.shape
+    rows = all_rows // expert_count
+    depth = expert_count // 4
+    half = width // group_count
+    columns = terms.shape[1]
+    dma = pltpu.SemaphoreType.DMA
+    whole = pl.BlockSpec(memory_space=pl.ANY)
+    held = pl.BlockSpec(memory_space=pltpu.VMEM)
+    half_type = jnp.bfloat16
+    return pl.pallas_call(
+        functools.partial(scatter_kernel, depth),
+        out_shape=[
+            jax.ShapeDtypeStruct((rows, half), half_type),
+            jax.ShapeDtypeStruct((columns // rank_width, half, rank_width), jnp.float32),
+        ],
+        in_specs=[whole] * 2,
+        out_specs=[held] * 2,
+        scratch_shapes=[
+            pltpu.VMEM((2 * depth, rows, width), half_type),
+            pltpu.VMEM((2 * depth, rows, width), half_type),
+            pltpu.VMEM((depth, rows, width), half_type),
+            pltpu.VMEM((depth, rows, width), half_type),
+            pltpu.VMEM((depth, rows, width), half_type),
+            pltpu.VMEM((rows, width), half_type),
+            pltpu.VMEM((rows, half), half_type),
+            pltpu.VMEM((half, columns), half_type),
+            pltpu.VMEM((half, columns), half_type),
+            dma((5,)),
+            dma((2, 4)),
+            dma((2, 4, depth)),
+            dma((2, 4, depth)),
+            dma((2, 4, depth)),
+            dma((2, 2)),
+            dma((2,)),
+        ],
+        compiler_params=pltpu.CompilerParams(collective_id=1, has_side_effects=True),
+    )(
+        part_rows.reshape(2 * depth, 2, rows, width),
+        terms.reshape(group_count, half, columns),
+    )
+
+
 def dense_form(
     saved_inputs, output_grad, routes, route_gates, expert_gate, expert_up, expert_down, proj_basis
 ):
-    model_width = saved_inputs.shape[1]
-    group_count = lax.axis_size("dp")
-    column_width = model_width // group_count
     experts = jnp.arange(LANES, dtype=jnp.int32)
     chosen = routes[:, :, None] == experts[None, None, :]
     gate_table = jnp.sum(
@@ -348,8 +559,6 @@
         lax.dot_general(grad_gate, gate_w, contract_last, preferred_element_type=jnp.float32)
         + lax.dot_general(grad_up, up_w, contract_last, preferred_element_type=jnp.float32)
     ).astype(jnp.bfloat16)
-    own_rows = lax.psum_scatter(part_rows, "expert", scatter_dimension=0, tiled=True)
-    token_grad = lax.psum_scatter(own_rows, "dp", scatter_dimension=1, tiled=True)
     coef_gate = jnp.dot(grad_gate, basis, preferred_element_type=jnp.float32).astype(jnp.bfloat16)
     coef_up = jnp.dot(grad_up, basis, preferred_element_type=jnp.float32).astype(jnp.bfloat16)
     coef_down = (gain * jnp.dot(hidden, basis, preferred_element_type=jnp.float32)).astype(
@@ -360,13 +569,9 @@
         input_rows, coef_pair, contract_first, preferred_element_type=jnp.float32
     )
     rear = lax.dot_general(grad_rows, coef_down, contract_first, preferred_element_type=jnp.float32)
-    summed_terms = lax.psum_scatter(
-        jnp.concatenate([front, rear], axis=1).astype(jnp.bfloat16),
-        "dp",
-        scatter_dimension=0,
-        tiled=True,
-    ).astype(jnp.float32)
-    projected = summed_terms.reshape(1, column_width, 3, rank_width)
+    terms = jnp.concatenate([front, rear], axis=1).astype(jnp.bfloat16)
+    token_grad, summed_terms = scatter_sums(part_rows, terms, rank_width)
+    projected = summed_terms.transpose(1, 0, 2)[None]
     return (token_grad, projected)
 
 

time: 268 us -> 200 us (0.75)
  waiting for transfers between devices: 131 us -> 0 us
  Pallas kernels: 63.3 us -> 136 us
  between operations: 13.9 us -> 0.77 us
  local copies, waits for them, and re-layouts: 4.48 us -> 7.95 us
    reduce_scatter x3 -> x0, waiting for transfers between devices: 131 us -> none  [the longest x1 75.7 us: dense_form(): lax.psum_scatter(part_rows, 'expert', scatter_dimension=0, tiled=True)]
    pallas_call x0 -> x1, Pallas kernels: none -> 72.2 us  [scatter_sums(): pl.pallas_call(functools.partial(scatter_kernel, depth), out_shape=[jax.S...]
    unnamed x18 -> x17, local copies, waits for them, and re-layouts: 3.72 us -> 7.19 us
    dot_general x1, matrix products: 6.3 us -> 9.49 us  [dense_form(): lax.dot_general(grad_rows, down_w, contract_last, preferred_element_type=...]
  transfers between devices with their start and end apart: 3 -> 0, of which waited for: 3 -> 0; matrix products, arithmetic and copies ran while one was open for 7% -> 0% of each run, Pallas kernels for 0% -> 0%
where the time goes in v3:
time: 200 us
  Pallas kernels  136 us (68%)
  matrix products  52.1 us (26%)
  local copies, waits for them, and re-layouts  7.95 us (4%)
  other arithmetic  3.89 us (2%)
    pallas_call x1, Pallas kernels, scatter_sums(): pl.pallas_call(functools.partial(scatter_kernel, depth), out_shape=[jax.S...  72.2 us
    pallas_call x1, Pallas kernels, gather_rows(): pl.pallas_call(functools.partial(gather_kernel, depth, split), out_shape=...  63.3 us
    dot_general x1, matrix products, dense_form(): lax.dot_general(grad_rows, down_w, contract_last, preferred_element_type=...  9.49 us
    dot_general x1, matrix products, dense_form(): lax.dot_general(grad_up, up_w, contract_last, preferred_element_type=jnp....  9.26 us
    dot_general x1, matrix products, dense_form(): pre_gate = jnp.dot(input_rows, gate_w, preferred_element_type=jnp.float32)  7.93 us
    dot_general x1, matrix products, dense_form(): lax.dot_general(grad_gate, gate_w, contract_last, preferred_element_type=...  7.37 us
    unnamed x17, local copies, waits for them, and re-layouts  7.19 us
    dot_general x1, matrix products, dense_form(): lax.dot_general(grad_rows, coef_down, contract_first, preferred_element_t...  6.66 us

profile of v3, /device:TPU:0, one launch (start us, length us, event | category | flops | bytes accessed | tf_op | source)
XLA Modules:
  0.0 200.2 jit_solution(15808646153429498921)
XLA Ops:
  0.6 0.0 copy-start
  0.7 0.8 copy.12
  1.5 0.8 copy.13
  2.2 0.8 select_reduce_fusion.1.g_in
  3.1 63.3 %shard_map.95 = (bf16[1024,3584]{1,0:T(8,128)(2,1)}, bf16[1024,3584]{1,0:T(8,128)(2,1)}, bf16[1024,128]{1,0:T(8,128)(2,1)}) custom-call(bf16[64,3584]{1,0:T(8,128)(2,1)} %x_in.1, bf16[64,3584]{1,0:T(8,128)(2,1)} %y_in.1, bf16[64,128]{1,0:T(8,128)(2,1)} %select_reduce_fusion.1.g_in), custom_call_target="tpu_custom_call" | custom-call | tf_op jit(solution)/shard_map/pallas_call | solution.py:288
  66.4 0.0 slice-start
  66.4 1.2 select_reduce_fusion
  67.7 0.0 slice-start.1
  67.7 0.0 copy-start.3
  67.7 7.9 %fusion.2 = f32[1024,512]{1,0:T(8,128)S(1)} fusion(bf16[1024,3584]{1,0:T(8,128)(2,1)} %get-tuple-element.9, bf16[1,3584,512]{2,1,0:T(8,128)(2,1)} %param.12), kind=kOutput, calls=%fused_computation.5 | convolution fusion | flops 3758096384 | bytes 13107200 | tf_op jit(solution)/shard_map/dot_general | solution.py:547
  75.6 0.0 slice-done
  75.6 0.0 slice-done.1
  75.6 0.0 copy-done.3
  75.7 5.3 %fusion.5 = f32[1024,512]{1,0:T(8,128)} fusion(bf16[1024,3584]{1,0:T(8,128)(2,1)S(1)} %bitcast.43, bf16[1,3584,512]{2,1,0:T(8,128)(2,1)S(1)} %copy-done.3), kind=kOutput, calls=%fused_computation.8 | convolution fusion | flops 3758096384 | bytes 13107200 | tf_op jit(solution)/shard_map/dot_general | solution.py:548
  80.9 0.0 copy-done
  80.9 6.7 %convolution_convert_fusion.1 = bf16[3584,128]{1,0:T(8,128)(2,1)S(1)} fusion(bf16[1024,3584]{1,0:T(8,128)(2,1)} %get-tuple-element.8, f32[1024,512]{1,0:T(8,128)} %fusion.5, f32[1024,512]{1,0:T(8,128)S(1)} %fusion.2, f32[1024]{0:T(1024)S(1)} %select_reduce_fusion, bf16[1,512,128]{2,1,0:T(8,128)(2,1)S(1)} %copy-done), kind=kOutput, calls=%fused_computation.2 | convolution fusion | flops 1077608448 | bytes 12587008 | tf_op jit(solution)/shard_map/dot_general | solution.py:571
  87.6 9.5 %multiply_convert_fusion.1 = (bf16[1024,512]{1,0:T(8,128)(2,1)S(1)}, bf16[1024,512]{1,0:T(8,128)(2,1)S(1)}) fusion(f32[1024]{0:T(1024)S(1)} %select_reduce_fusion, f32[1024,512]{1,0:T(8,128)S(1)} %fusion.2, f32[1024,512]{1,0:T(8,128)} %fusion.5, bf16[1024,3584]{1,0:T(8,128)(2,1)} %get-tuple-element.8, bf16[1,512,3584]{2,1,0:T(8,128)(2,1)} %param.14), kind=kOutput, calls=%fused_computation.14 | convolution fusion | flops 3765436416 | bytes 17305600 | tf_op jit(solution)/shard_map/dot_general | solution.py:549
  97.1 0.4 convolution_convert_fusion.2
  97.5 0.4 convolution_convert_fusion.3
  98.0 5.2 %convolution_convert_fusion = bf16[3584,256]{1,0:T(8,128)(2,1)S(1)} fusion(bf16[1024,3584]{1,0:T(8,128)(2,1)} %get-tuple-element.9, bf16[1024,128]{1,0:T(8,128)(2,1)S(1)} %convolution_convert_fusion.2, bf16[1024,128]{1,0:T(8,128)(2,1)S(1)} %convolution_convert_fusion.3), kind=kOutput, calls=%fused_computation.1 | convolution fusion | flops 1881014272 | bytes 9699328 | tf_op jit(solution)/shard_map/dot_general | solution.py:568
  103.2 0.0 copy-start.2
  103.2 1.8 pad_maximum_fusion.terms
  105.0 1.2 copy-done.2
  106.2 0.0 copy-start.4
  106.2 7.4 %fusion = f32[1024,3584]{1,0:T(8,128)} fusion(bf16[1024,512]{1,0:T(8,128)(2,1)S(1)} %get-tuple-element.13, bf16[1,3584,512]{2,1,0:T(8,128)(2,1)S(1)} %copy-done.2), kind=kOutput, calls=%fused_computation.3 | convolution fusion | flops 3758096384 | bytes 19398656 | tf_op jit(solution)/shard_map/dot_general | solution.py:559
  113.6 0.0 copy-done.4
  113.6 9.3 %add_convert_fusion = bf16[1024,3584]{1,0:T(8,128)(2,1)} fusion(f32[1024,3584]{1,0:T(8,128)} %fusion, bf16[1024,512]{1,0:T(8,128)(2,1)S(1)} %get-tuple-element.12, bf16[1,3584,512]{2,1,0:T(8,128)(2,1)S(1)} %copy-done.4), kind=kOutput, calls=%fused_computation | convolution fusion | flops 3765436416 | bytes 26738688 | tf_op jit(solution)/shard_map/dot_general | solution.py:560
  122.9 0.0 copy-start.1
  122.9 72.2 %shard_map.96 = (bf16[64,1792]{1,0:T(8,128)(2,1)}, f32[3,1792,128]{2,1,0:T(8,128)}) custom-call(bf16[8,2,64,3584]{3,2,1,0:T(8,128)(2,1)} %bitcast.38, bf16[2,1792,384]{2,1,0:T(8,128)(2,1)} %pad_maximum_fusion.terms), custom_call_target="tpu_custom_call" | custom-call | tf_op jit(solution)/shard_map/pallas_call | solution.py:494
  195.0 1.6 copy.16
  196.7 3.5 %copy.17 = f32[1,1792,3,128]{3,1,2,0:T(8,128)} copy(f32[1,1792,3,128]{3,1,2,0:T(8,128)} %bitcast.39) | data formatting | bytes 5505024
  200.2 0.0 copy-done.1
  (2 shorter events, 0.0 us)
Async XLA Ops:
  0.6 80.3 %copy-start = (bf16[1,512,128]{2,1,0:T(8,128)(2,1)S(1)}, bf16[1,512,128]{2,1,0:T(8,128)(2,1)}, u32[]{:S(2)}) copy-start(bf16[1,512,128]{2,1,0:T(8,128)(2,1)} %param.15) | copy-start | bytes 393220
  66.4 9.2 %slice-start = ((s8[7340032]{0:T(1024)(128)(4,1)}), s8[4194304]{0:T(1024)(128)(4,1)S(1)}, s32[]{:S(2)}) async-start(s8[7340032]{0:T(1024)(128)(4,1)} %bitcast.42), calls=%async_computation | async-start | bytes 8388608
  67.7 8.0 %slice-start.1 = ((s8[7340032]{0:T(1024)(128)(4,1)}), s8[3145728]{0:T(1024)(128)(4,1)S(1)}, s32[]{:S(2)}) async-start(s8[7340032]{0:T(1024)(128)(4,1)} %bitcast.42), calls=%async_computation.1 | async-start | bytes 6291456
  67.7 8.0 %copy-start.3 = (bf16[1,3584,512]{2,1,0:T(8,128)(2,1)S(1)}, bf16[1,3584,512]{2,1,0:T(8,128)(2,1)}, u32[]{:S(2)}) copy-start(bf16[1,3584,512]{2,1,0:T(8,128)(2,1)} %param.13) | copy-start | bytes 11010052
  103.2 3.0 %copy-start.2 = (bf16[1,3584,512]{2,1,0:T(8,128)(2,1)S(1)}, bf16[1,3584,512]{2,1,0:T(8,128)(2,1)}, u32[]{:S(2)}) copy-start(bf16[1,3584,512]{2,1,0:T(8,128)(2,1)} %param.12) | copy-start | bytes 11010052
  106.2 7.4 %copy-start.4 = (bf16[1,3584,512]{2,1,0:T(8,128)(2,1)S(1)}, bf16[1,3584,512]{2,1,0:T(8,128)(2,1)}, u32[]{:S(2)}) copy-start(bf16[1,3584,512]{2,1,0:T(8,128)(2,1)} %param.13) | copy-start | bytes 11010052
  122.9 77.3 %copy-start.1 = (bf16[1,512,128]{2,1,0:T(8,128)(2,1)S(1)}, bf16[1,512,128]{2,1,0:T(8,128)(2,1)}, u32[]{:S(2)}) copy-start(bf16[1,512,128]{2,1,0:T(8,128)(2,1)} %param.15) | copy-start | bytes 393220
